TPU v7x, 32 devices: a whole 2x2x4 slice. The times are simulated.
32 devices in a mesh: rep: 8 (over z, x), shard: 4 (over y, core).
Axes of the slice: x: 2, y: 2, z: 4, core: 2. Of those that a mesh axis runs over, the one named last changes fastest.
Arguments:
- grads: bfloat16 [8, 12, 512, 512], P('rep', 'shard')
- owner_slot: int32 [12], replicated, may hold values from 0 to 11, as said below
- refresh: int32 [1], replicated, may hold values from 0 to 11
- left_stat: float32 [12, 512, 512], P('shard', 'rep'), as said below
- right_stat: float32 [12, 512, 512], P('shard', 'rep'), as said below
- left_root: bfloat16 [12, 512, 512], P('shard', 'rep'), as said below
- right_root: bfloat16 [12, 512, 512], P('shard'), as said below
Outputs:
- left_new: float32 [12, 512, 512], P('shard', 'rep')
- right_new: float32 [12, 512, 512], P('shard', 'rep')
- left_root_new: bfloat16 [12, 512, 512], P('shard', 'rep')
- right_root_new: bfloat16 [12, 512, 512], P('shard')
- direction: bfloat16 [12, 512, 512], P('shard')
Inputs may be any that keep to these rules, and one draw needn't show every extreme that they name: A permutation: block b sits at position owner_slot[b] of owner order, which belongs to shard index owner_slot[b] // 3, with owner_slot[b] % 3 == b % 3; the 3 blocks s * 3 to s * 3 + 2 all go to different shard indices. `left_stat`: each block is symmetric positive definite. `right_stat`: each block is symmetric positive definite. `left_root`: each block is symmetric. `right_root`: each block is symmetric.
All inputs are finite; a program needn't handle non-finite values.
Results may differ from a plain program's by a relative error of at most 0.0004.
The roundings to bfloat16 on the way count: a program that leaves them out, or rounds other values in their place, can miss the bound.
Values may be sent and summed in bfloat16 or wider, within the bound.
A program may use at most 64 MiB of HBM per device.

v0:
```python
import jax
import jax.numpy as jnp
from jax import lax
from jax.sharding import PartitionSpec as P

ITERS = 2


decay_rate = 0.95
epsilon_shift = 1e-06


def inverse_root(statistic):
    order = statistic.shape[0]
    identity = jnp.eye(order, dtype=jnp.float32)
    shifted = statistic + epsilon_shift * identity
    norm_scale = 2.5 / jnp.sqrt(jnp.sum(shifted * shifted))
    moment = norm_scale * shifted
    current = identity
    for number in range(ITERS):
        factor = (5.0 * identity - moment) * 0.25
        factor_low = factor.astype(jnp.bfloat16)
        if number == 0:
            current = jnp.sqrt(jnp.sqrt(norm_scale)) * factor
        else:
            current = jnp.dot(
                current.astype(jnp.bfloat16), factor_low, preferred_element_type=jnp.float32
            )
        if number + 1 < ITERS:
            square = jnp.dot(factor_low, factor_low, preferred_element_type=jnp.float32).astype(
                jnp.bfloat16
            )
            fourth = jnp.dot(square, square, preferred_element_type=jnp.float32).astype(
                jnp.bfloat16
            )
            moment = jnp.dot(
                fourth, moment.astype(jnp.bfloat16), preferred_element_type=jnp.float32
            )
    return current.astype(jnp.bfloat16)


def both_roots(fresh_whole):
    return (inverse_root(fresh_whole[0]), inverse_root(fresh_whole[1]))


def empty_roots(fresh_whole):
    blank = jnp.zeros(fresh_whole.shape[1:], jnp.bfloat16)
    return (blank, blank)


def body(grads, owner_slot, refresh, left_stat, right_stat, left_root, right_root):
    blocks = grads.shape[1]
    block_order = grads.shape[2]
    rep_count = lax.axis_size("rep")
    shards = lax.axis_size("shard")
    row_count = block_order // rep_count
    rep_index = lax.axis_index("rep")
    shard_index = lax.axis_index("shard")
    partial_value = grads[0].astype(jnp.float32)
    row_share = lax.psum_scatter(partial_value, "rep", scatter_dimension=1, tiled=True)
    row_share = row_share.astype(jnp.bfloat16)
    slot_table = owner_slot.reshape(shards, blocks)
    own_slots = lax.dynamic_index_in_dim(slot_table, shard_index, 0, keepdims=False)
    targets = own_slots // blocks
    selector = (targets[None, :] == jnp.arange(shards, dtype=jnp.int32)[:, None]).astype(
        jnp.bfloat16
    )
    outgoing = jnp.einsum(
        "ok,krc->orc", selector, row_share, preferred_element_type=jnp.float32
    ).astype(jnp.bfloat16)
    incoming = lax.all_to_all(outgoing, "shard", split_axis=0, concat_axis=0, tiled=True)
    wanted = shard_index * blocks + jnp.arange(blocks, dtype=jnp.int32)
    receiver = (jnp.transpose(slot_table) == wanted[:, None]).astype(jnp.bfloat16)
    owned_rows = jnp.einsum(
        "ks,src->krc", receiver, incoming, preferred_element_type=jnp.float32
    ).astype(jnp.bfloat16)
    gathered = lax.all_gather(owned_rows, "rep", axis=1, tiled=True)
    left_new = (
        decay_rate * left_stat
        + jnp.einsum("krc,kjc->krj", owned_rows, gathered, preferred_element_type=jnp.float32)
        / block_order
    )
    column_share = lax.dynamic_slice_in_dim(gathered, rep_index * row_count, row_count, 2)
    right_new = (
        decay_rate * right_stat
        + jnp.einsum("kic,kij->kcj", column_share, gathered, preferred_element_type=jnp.float32)
        / block_order
    )
    fresh_slot = owner_slot[refresh[0]]
    holder = fresh_slot // blocks
    slot_index = fresh_slot % blocks
    owns_fresh = holder == shard_index
    fresh_pair = jnp.stack(
        [
            lax.dynamic_index_in_dim(left_new, slot_index, 0, keepdims=False),
            lax.dynamic_index_in_dim(right_new, slot_index, 0, keepdims=False),
        ]
    )
    fresh_whole = lax.all_gather(fresh_pair, "rep", axis=1, tiled=True)
    fresh_left, fresh_right = lax.cond(owns_fresh, both_roots, empty_roots, fresh_whole)
    fresh_rows = lax.dynamic_slice_in_dim(fresh_left, rep_index * row_count, row_count, 0)
    left_updated = lax.dynamic_update_index_in_dim(left_root, fresh_rows, slot_index, 0)
    left_root_new = jnp.where(owns_fresh, left_updated, left_root)
    right_updated = lax.dynamic_update_index_in_dim(right_root, fresh_right, slot_index, 0)
    right_root_new = jnp.where(owns_fresh, right_updated, right_root)
    half_step = jnp.einsum(
        "kri,kic->krc", left_root_new, gathered, preferred_element_type=jnp.float32
    ).astype(jnp.bfloat16)
    preconditioned = jnp.einsum(
        "kri,kic->krc", half_step, right_root_new, preferred_element_type=jnp.float32
    ).astype(jnp.bfloat16)
    direction = lax.all_gather(preconditioned, "rep", axis=1, tiled=True)
    return (left_new, right_new, left_root_new, right_root_new, direction)


def solution(mesh):
    return jax.shard_map(
        body,
        mesh=mesh,
        in_specs=(
            P("rep", "shard", None, None),
            P(),
            P(),
            P("shard", "rep", None),
            P("shard", "rep", None),
            P("shard", "rep", None),
            P("shard", None, None),
        ),
        out_specs=(
            P("shard", "rep", None),
            P("shard", "rep", None),
            P("shard", "rep", None),
            P("shard", None, None),
            P("shard", None, None),
        ),
        check_vma=False,
    )
```

profile of v0, /device:TPU:25, one launch (start us, length us, event | category | flops | bytes accessed | tf_op | source)
XLA Modules:
  0.0 267.2 jit_solution(3963300385175303924)
XLA Ops:
  7.2 0.0 copy-start.3
  7.2 0.0 reduce-scatter.2.cloned.1.call-start
  7.2 1.4 copy-done.3
  8.6 2.1 bitcast_convert_fusion
  10.7 0.0 reduce-scatter.2.cloned.1.call-update
  10.7 0.6 copy-done.10
  11.3 0.1 reshape.53
  11.4 73.3 %reduce-scatter.2.cloned.1.call-done = f32[3,64,512]{2,1,0:T(8,128)} async-done(((f32[3,512,512]{2,1,0:T(8,128)}), f32[3,64,512]{2,1,0:T(8,128)}) %reduce-scatter.2.cloned.1.call-update) | async-done | bytes 393232 | tf_op jit(solution)/shard_map/reduce_scatter | solution.py:60
  84.7 1.0 convert_element_type.80
  85.7 0.0 copy-start.8
  85.8 0.3 convolution_convert_fusion.6
  86.1 0.7 copy.23
  86.8 5.1 %all-to-all-start = ((bf16[4,64,512]{2,1,0:T(8,128)(2,1)}), bf16[4,64,512]{2,1,0:T(8,128)(2,1)S(1)}, u32[]{:S(2)}, u32[]{:S(2)}) async-start(bf16[4,64,512]{2,1,0:T(8,128)(2,1)} %copy.23), calls=%async_computation.1 | async-start | bytes 524288 | tf_op jit(solution)/shard_map/all_to_all | solution.py:71
  91.9 0.0 all-gather.4.cloned.1.call-start
  91.9 5.0 %all-to-all-done = bf16[4,64,512]{2,1,0:T(8,128)(2,1)S(1)} async-done(((bf16[4,64,512]{2,1,0:T(8,128)(2,1)}), bf16[4,64,512]{2,1,0:T(8,128)(2,1)S(1)}, u32[]{:S(2)}, u32[]{:S(2)}) %all-to-all-start) | async-done | bytes 262176 | tf_op jit(solution)/shard_map/all_to_all | solution.py:71
  96.9 0.4 fusion.92
  97.3 0.0 copy-start.9
  97.3 0.7 copy.36
  98.0 0.0 all-gather.4.cloned.1.call-update
  98.0 0.0 all-gather.6.cloned.1.call-start
  98.8 0.6 dynamic_slice.22
  100.0 40.3 %all-gather.4.cloned.1.call-done = bf16[3,512,512]{2,1,0:T(8,128)(2,1)} async-done(((bf16[3,64,512]{2,1,0:T(8,128)(2,1)}), bf16[3,512,512]{2,1,0:T(8,128)(2,1)}) %all-gather.4.cloned.1.call-update) | async-done | bytes 1572880 | tf_op jit(solution)/shard_map/all_gather | solution.py:77
  140.3 0.0 copy-done.8
  140.3 2.2 fusion.90
  142.5 0.0 copy-done.9
  142.5 0.0 copy-done
  142.5 0.0 copy-start.6
  142.6 0.5 fusion.89
  143.1 0.2 copy-done.6
  143.3 0.7 copy-done.7
  144.0 0.7 pad_maximum_fusion
  144.8 0.0 all-gather.6.cloned.1.call-update
  144.8 0.0 all-gather.8.cloned.1.call-start
  146.1 0.0 copy-start.2
  146.2 46.4 %all-gather.6.cloned.1.call-done = f32[2,512,512]{2,1,0:T(8,128)} async-done(((f32[2,64,512]{2,1,0:T(8,128)}), f32[2,512,512]{2,1,0:T(8,128)}) %all-gather.6.cloned.1.call-update) | async-done | bytes 2097168 | tf_op jit(solution)/shard_map/all_gather | solution.py:99
  192.5 1.7 conditional.1
  192.5 0.8 broadcast.90
  193.3 0.8 broadcast_in_dim.12
  194.2 0.2 select_dynamic-update-slice_fusion
  194.4 0.0 copy-start.1
  194.4 0.7 copy-done.5
  195.1 0.9 fusion.95
  196.0 0.0 copy-start.4
  196.0 1.3 convolution_convert_fusion.7
  197.3 0.0 copy-done.4
  197.3 0.0 all-gather.8.cloned.1.call-update
  197.3 60.6 %all-gather.8.cloned.1.call-done = bf16[3,512,512]{2,1,0:T(8,128)(2,1)} async-done(((bf16[3,64,512]{2,1,0:T(8,128)(2,1)}), bf16[3,512,512]{2,1,0:T(8,128)(2,1)}) %all-gather.8.cloned.1.call-update) | async-done | bytes 1572880 | tf_op jit(solution)/shard_map/all_gather | solution.py:112
  258.0 2.7 copy.49
  (9 shorter events, 0.0 us)
Async XLA Ops:
  7.2 1.4 copy-start.3
  7.2 77.6 %reduce-scatter.2.cloned.1.call-start = ((), (), s32[]{:S(2)}) async-start(), calls=%async_computation.2 | async-start | bytes 3538944 | tf_op jit(solution)/shard_map/reduce_scatter | solution.py:60
  10.7 0.7 copy-start.10
  85.7 54.6 %copy-start.8 = (f32[3,64,512]{2,1,0:T(8,128)S(1)}, f32[3,64,512]{2,1,0:T(8,128)}, u32[]{:S(2)}) copy-start(f32[3,64,512]{2,1,0:T(8,128)} %param.12) | copy-start | bytes 1179652
  86.8 10.1 %all-to-all-start = ((bf16[4,64,512]{2,1,0:T(8,128)(2,1)}), bf16[4,64,512]{2,1,0:T(8,128)(2,1)S(1)}, u32[]{:S(2)}, u32[]{:S(2)}) async-start(bf16[4,64,512]{2,1,0:T(8,128)(2,1)} %copy.23), calls=%async_computation.1 | async-start | bytes 524288 | tf_op jit(solution)/shard_map/all_to_all | solution.py:71
  91.9 48.4 %all-gather.4.cloned.1.call-start = ((), (), s32[]{:S(2)}) async-start(), calls=%async_computation.3 | async-start | bytes 1769472 | tf_op jit(solution)/shard_map/all_gather | solution.py:77
  97.3 45.2 %copy-start.9 = (f32[3,64,512]{2,1,0:T(8,128)S(1)}, f32[3,64,512]{2,1,0:T(8,128)}, u32[]{:S(2)}) copy-start(f32[3,64,512]{2,1,0:T(8,128)} %param.13) | copy-start | bytes 1179652
  98.0 94.5 %all-gather.6.cloned.1.call-start = ((), (), s32[]{:S(2)}) async-start(), calls=%async_computation.4 | async-start | bytes 2359296 | tf_op jit(solution)/shard_map/all_gather | solution.py:99
  140.3 2.2 copy-start
  142.5 0.7 copy-start.6
  143.3 0.7 copy-start.7
  144.8 113.2 %all-gather.8.cloned.1.call-start = ((), (), s32[]{:S(2)}) async-start(), calls=%async_computation.5 | async-start | bytes 1769472 | tf_op jit(solution)/shard_map/all_gather | solution.py:112
  146.1 48.0 %copy-start.2 = (bf16[3,512,512]{2,1,0:T(8,128)(2,1)S(1)}, bf16[3,512,512]{2,1,0:T(8,128)(2,1)}, u32[]{:S(2)}) copy-start(bf16[3,512,512]{2,1,0:T(8,128)(2,1)} %param.15) | copy-start | bytes 4718596
  194.2 0.9 copy-start.5
  194.4 3.0 %copy-start.1 = (bf16[3,512,512]{2,1,0:T(8,128)(2,1)}, bf16[3,512,512]{2,1,0:T(8,128)(2,1)S(1)}, u32[]{:S(2)}) copy-start(bf16[3,512,512]{2,1,0:T(8,128)(2,1)S(1)} %select_dynamic-update-slice_fusion) | copy-start | bytes 4718596
  196.0 1.4 copy-start.4
Sparse Core Ops, SparseCore 0:
  11.6 73.0 reduce-scatter.1
  98.2 42.0 all-gather.3
  144.9 47.5 all-gather.5
  197.5 60.4 all-gather.7
where the time goes:
time: 272 us; the launch traced here: 267 us
  waiting for transfers between devices  226 us (83%)
  between operations  16.5 us (6%)
  local copies, waits for them, and re-layouts  10.1 us (4%)
  starting transfers between devices  5.21 us (2%)
  other arithmetic  4.88 us (2%)
  matrix products  4.74 us (2%)
    reduce_scatter x1, waiting for transfers between devices, body(): lax.psum_scatter(partial_value, 'rep', scatter_dimension=1, tiled=True)  73.3 us
    all_gather x1, waiting for transfers between devices, body(): direction = lax.all_gather(preconditioned, 'rep', axis=1, tiled=True)  60.6 us
    all_gather x1, waiting for transfers between devices, body(): fresh_whole = lax.all_gather(fresh_pair, 'rep', axis=1, tiled=True)  46.4 us
    all_gather x1, waiting for transfers between devices, body(): gathered = lax.all_gather(owned_rows, 'rep', axis=1, tiled=True)  40.3 us
    unnamed x23, local copies, waits for them, and re-layouts  6.3 us
  transfers between devices with their start and end apart: 5, of which 5 were waited for; matrix products, arithmetic and copies ran while one was open for 0% of the time, Pallas kernels for 0%

commit v1 on v0

--- a/solution.py
+++ b/solution.py
@@ -1,6 +1,10 @@
+import functools
+
 import jax
 import jax.numpy as jnp
 from jax import lax
+from jax.experimental import pallas as pl
+from jax.experimental.pallas import tpu as pltpu
 from jax.sharding import PartitionSpec as P
 
 ITERS = 2
@@ -113,7 +117,312 @@
     return (left_new, right_new, left_root_new, right_root_new, direction)
 
 
+MESH = pl.DeviceIdType.MESH
+
+
+def exchange_kernel(
+    reps,
+    shards,
+    slots_ref,
+    grads_ref,
+    left_ref,
+    stat_ref,
+    owned_ref,
+    grad_full,
+    left_full,
+    stat_full,
+    pieces,
+    share,
+    outgoing,
+    incoming,
+    sum_send,
+    sum_recv,
+    swap_send,
+    swap_recv,
+    line_send,
+    line_recv,
+    local_sem,
+):
+    blocks = grads_ref.shape[1]
+    rows = grads_ref.shape[2] // reps
+    length = reps // 2
+    me = lax.axis_index("rep")
+    shard = lax.axis_index("shard")
+    place = me // 2
+    side = me % 2
+    partner = place * 2 + (1 - side)
+
+    def span(index):
+        return pl.ds(pl.multiple_of(index * rows, rows), rows)
+
+    barrier = pltpu.get_barrier_semaphore()
+    for step in range(1, reps):
+        pl.semaphore_signal(
+            barrier, inc=1, device_id=((me + step) % reps, shard), device_id_type=MESH
+        )
+    for step in range(1, shards):
+        pl.semaphore_signal(
+            barrier, inc=1, device_id=(me, (shard + step) % shards), device_id_type=MESH
+        )
+    pl.semaphore_wait(barrier, reps + shards - 2)
+
+    sums = []
+    for step in SUM_ORDER(reps):
+        peer = (me + step) % reps
+        copy = pltpu.make_async_remote_copy(
+            src_ref=grads_ref.at[0, :, span(peer), :],
+            dst_ref=pieces.at[me],
+            send_sem=sum_send.at[step],
+            recv_sem=sum_recv.at[step],
+            device_id=(peer, shard),
+            device_id_type=MESH,
+        )
+        copy.start()
+        sums.append(copy)
+
+    fulls = (left_full, stat_full, grad_full)
+
+    def line_copy(array, source, way, target, first):
+        full = fulls[array]
+        origin = first if first is not None else full.at[:, span(source), :]
+        return pltpu.make_async_remote_copy(
+            src_ref=origin,
+            dst_ref=full.at[:, span(source), :],
+            send_sem=line_send.at[array, source, way],
+            recv_sem=line_recv.at[array, source],
+            device_id=(target, shard),
+            device_id_type=MESH,
+        )
+
+    ways = ((0, 1), (1, -1))
+
+    def send_line(array, source, way, delta, first):
+        inside = (place + delta >= 0) & (place + delta < length)
+
+        @pl.when(inside)
+        def _():
+            line_copy(array, source, way, me + 2 * delta, first).start()
+
+    def wait_line(array, source, way, delta, first):
+        inside = (place + delta >= 0) & (place + delta < length)
+
+        @pl.when(inside)
+        def _():
+            line_copy(array, source, way, me + 2 * delta, first).wait_send()
+
+    def begin(array, first):
+        for way, delta in ways:
+            send_line(array, me, way, delta, first)
+        line_copy(array, me, 2, partner, first).start()
+
+    def forward(array, hop):
+        for way, delta in ways:
+            origin = place - delta * hop
+
+            @pl.when((origin >= 0) & (origin < length))
+            def _():
+                source = origin * 2 + side
+                line_copy(array, source, 2, partner, None).wait_recv()
+                send_line(array, source, way, delta, None)
+                line_copy(array, source, 2, partner, None).start()
+
+    def finish(array, first):
+        for other in range(length):
+            line_copy(array, other * 2 + 1 - side, 2, partner, None).wait_recv()
+        for way, delta in ways:
+            wait_line(array, me, way, delta, first)
+        line_copy(array, me, 2, partner, first).wait_send()
+        for hop in range(1, length):
+            for way, delta in ways:
+                origin = place - delta * hop
+
+                @pl.when((origin >= 0) & (origin < length))
+                def _():
+                    source = origin * 2 + side
+                    wait_line(array, source, way, delta, None)
+                    line_copy(array, source, 2, partner, None).wait_send()
+
+    begin(0, left_ref)
+    begin(1, stat_ref)
+    own_left = pltpu.make_async_copy(left_ref, left_full.at[:, span(me), :], local_sem.at[0])
+    own_left.start()
+    own_stat = pltpu.make_async_copy(stat_ref, stat_full.at[:, span(me), :], local_sem.at[1])
+    own_stat.start()
+
+    pieces[me] = grads_ref[0, :, span(me), :]
+    for copy in sums:
+        copy.wait_recv()
+    for block in range(blocks):
+        total = pieces[0, block].astype(jnp.float32)
+        for index in range(1, reps):
+            total = total + pieces[index, block].astype(jnp.float32)
+        share[block] = total.astype(jnp.bfloat16)
+
+    for target in range(shards):
+        chosen = jnp.int32(0)
+        for block in range(1, blocks):
+            chosen = jnp.where(
+                slots_ref[shard * blocks + block] // blocks == target, jnp.int32(block), chosen
+            )
+        outgoing[target] = share[chosen]
+    swaps = []
+    for step in range(1, shards):
+        peer = (shard + step) % shards
+        copy = pltpu.make_async_remote_copy(
+            src_ref=outgoing.at[peer],
+            dst_ref=incoming.at[shard],
+            send_sem=swap_send.at[step],
+            recv_sem=swap_recv.at[step],
+            device_id=(me, peer),
+            device_id_type=MESH,
+        )
+        copy.start()
+        swaps.append(copy)
+    incoming[shard] = outgoing[shard]
+    for copy in swaps:
+        copy.wait_recv()
+    for block in range(blocks):
+        holder = jnp.int32(0)
+        for origin in range(1, shards):
+            holder = jnp.where(
+                slots_ref[origin * blocks + block] == shard * blocks + block,
+                jnp.int32(origin),
+                holder,
+            )
+        value = incoming[holder]
+        owned_ref[block] = value
+        grad_full[block, span(me), :] = value
+    begin(2, owned_ref)
+    for hop in range(1, length):
+        for array in range(3):
+            forward(array, hop)
+    for array, first in enumerate((left_ref, stat_ref, owned_ref)):
+        finish(array, first)
+    own_left.wait()
+    own_stat.wait()
+    for copy in sums + swaps:
+        copy.wait_send()
+
+
+def SUM_ORDER(reps):
+    return range(1, reps)
+
+
+def exchange(owner_slot, grads, left_root, fresh_stats, reps, shards):
+    blocks, order = grads.shape[1], grads.shape[2]
+    rows = order // reps
+    low = jnp.bfloat16
+    vmem = pl.BlockSpec(memory_space=pltpu.VMEM)
+    return pl.pallas_call(
+        functools.partial(exchange_kernel, reps, shards),
+        out_shape=(
+            jax.ShapeDtypeStruct((blocks, rows, order), low),
+            jax.ShapeDtypeStruct((blocks, order, order), low),
+            jax.ShapeDtypeStruct((blocks, order, order), low),
+            jax.ShapeDtypeStruct((2, order, order), low),
+        ),
+        in_specs=[pl.BlockSpec(memory_space=pltpu.SMEM), vmem, vmem, vmem],
+        out_specs=(vmem, vmem, vmem, vmem),
+        scratch_shapes=[
+            pltpu.VMEM((reps, blocks, rows, order), low),
+            pltpu.VMEM((blocks, rows, order), low),
+            pltpu.VMEM((shards, rows, order), low),
+            pltpu.VMEM((shards, rows, order), low),
+            pltpu.SemaphoreType.DMA((reps,)),
+            pltpu.SemaphoreType.DMA((reps,)),
+            pltpu.SemaphoreType.DMA((shards,)),
+            pltpu.SemaphoreType.DMA((shards,)),
+            pltpu.SemaphoreType.DMA((3, reps, 3)),
+            pltpu.SemaphoreType.DMA((3, reps)),
+            pltpu.SemaphoreType.DMA((2,)),
+        ],
+        compiler_params=pltpu.CompilerParams(collective_id=0, has_side_effects=True),
+    )(owner_slot, grads, left_root, fresh_stats)
+
+
+def direct_body(grads, owner_slot, refresh, left_stat, right_stat, left_root, right_root):
+    blocks = grads.shape[1]
+    block_order = grads.shape[2]
+    rep_count = lax.axis_size("rep")
+    shards = lax.axis_size("shard")
+    row_count = block_order // rep_count
+    rep_index = lax.axis_index("rep")
+    shard_index = lax.axis_index("shard")
+    fresh_slot = owner_slot[refresh[0]]
+    slot_index = fresh_slot % blocks
+    owns_fresh = fresh_slot // blocks == shard_index
+    fresh_stats = jnp.stack(
+        [
+            lax.dynamic_index_in_dim(left_stat, slot_index, 0, keepdims=False),
+            lax.dynamic_index_in_dim(right_stat, slot_index, 0, keepdims=False),
+        ]
+    ).astype(jnp.bfloat16)
+    owned_rows, gathered, left_full, stat_full = exchange(
+        owner_slot, grads, left_root, fresh_stats, rep_count, shards
+    )
+    left_new = (
+        decay_rate * left_stat
+        + jnp.einsum("krc,kjc->krj", owned_rows, gathered, preferred_element_type=jnp.float32)
+        / block_order
+    )
+    column_share = lax.dynamic_slice_in_dim(gathered, rep_index * row_count, row_count, 2)
+    right_new = (
+        decay_rate * right_stat
+        + jnp.einsum("kic,kij->kcj", column_share, gathered, preferred_element_type=jnp.float32)
+        / block_order
+    )
+    grad_fresh = lax.dynamic_index_in_dim(gathered, slot_index, 0, keepdims=False)
+
+    def renew(operands):
+        grad, stats = operands
+        wide = stats.astype(jnp.float32)
+        left = (
+            decay_rate * wide[0]
+            + jnp.einsum("ic,jc->ij", grad, grad, preferred_element_type=jnp.float32) / block_order
+        )
+        right = (
+            decay_rate * wide[1]
+            + jnp.einsum("ci,cj->ij", grad, grad, preferred_element_type=jnp.float32) / block_order
+        )
+        return inverse_root(left), inverse_root(right)
+
+    def skip(operands):
+        blank = jnp.zeros((block_order, block_order), jnp.bfloat16)
+        return blank, blank
+
+    fresh_left, fresh_right = lax.cond(owns_fresh, renew, skip, (grad_fresh, stat_full))
+    left_all = jnp.where(
+        owns_fresh, lax.dynamic_update_index_in_dim(left_full, fresh_left, slot_index, 0), left_full
+    )
+    fresh_rows = lax.dynamic_slice_in_dim(fresh_left, rep_index * row_count, row_count, 0)
+    left_updated = lax.dynamic_update_index_in_dim(left_root, fresh_rows, slot_index, 0)
+    left_root_new = jnp.where(owns_fresh, left_updated, left_root)
+    right_updated = lax.dynamic_update_index_in_dim(right_root, fresh_right, slot_index, 0)
+    right_root_new = jnp.where(owns_fresh, right_updated, right_root)
+    half_step = jnp.einsum(
+        "kri,kic->krc", left_all, gathered, preferred_element_type=jnp.float32
+    ).astype(jnp.bfloat16)
+    direction = jnp.einsum(
+        "kri,kic->krc", half_step, right_root_new, preferred_element_type=jnp.float32
+    ).astype(jnp.bfloat16)
+    return (left_new, right_new, left_root_new, right_root_new, direction)
+
+
+def choose(mesh, *arrays):
+    reps = mesh.shape["rep"]
+    rows = arrays[0].shape[2] // reps
+    direct = reps % 2 == 0 and rows % 16 == 0
+    return (direct_body if direct else body)
+
+
 def solution(mesh):
+    def run(*arrays):
+        return mapped(mesh, choose(mesh, *arrays))(*arrays)
+
+    return run
+
+
+def mapped(mesh, body):
     return jax.shard_map(
         body,
         mesh=mesh,

time: 272 us -> 135 us (0.50); the launches traced: 267 us -> 135 us
  waiting for transfers between devices: 226 us -> 0 us
  Pallas kernels: 0 us -> 88.6 us
  matrix products: 4.74 us -> 30 us
  between operations: 16.5 us -> 3.34 us
  starting transfers between devices: 5.21 us -> 0 us
  local copies, waits for them, and re-layouts: 10.1 us -> 5.95 us
    all_gather x3 -> x0, waiting for transfers between devices: 147 us -> none  [the longest x1 60.6 us: body(): direction = lax.all_gather(preconditioned, 'rep', axis=1, tiled=True)]
    pallas_call x0 -> x1, Pallas kernels: none -> 88.6 us  [exchange(): pl.pallas_call(functools.partial(exchange_kernel, reps, shards), out_shap...]
    reduce_scatter x1 -> x0, waiting for transfers between devices: 73.3 us -> none  [body(): lax.psum_scatter(partial_value, 'rep', scatter_dimension=1, tiled=True)]
    dot_general x5 -> x9, matrix products: 4.74 us -> 30 us  [the longest x2 9.09 us: inverse_root(): jnp.dot(square, square, preferred_element_type=jnp.float32)]
    all_to_all x1 -> x0, starting transfers between devices: 5.08 us -> none  [body(): lax.all_to_all(outgoing, 'shard', split_axis=0, concat_axis=0, tiled=True)]
    all_to_all x1 -> x0, waiting for transfers between devices: 5.03 us -> none  [body(): lax.all_to_all(outgoing, 'shard', split_axis=0, concat_axis=0, tiled=True)]
    unnamed x23 -> x15, local copies, waits for them, and re-layouts: 6.3 us -> 1.65 us
  transfers between devices with their start and end apart: 5 -> 0, of which waited for: 5 -> 0; matrix products, arithmetic and copies ran while one was open for 0% -> 0% of each run, Pallas kernels for 0% -> 0%
where the time goes in v1:
time: 135 us
  Pallas kernels  88.6 us (66%)
  matrix products  30 us (22%)
  local copies, waits for them, and re-layouts  5.95 us (4%)
  other arithmetic  5.7 us (4%)
  between operations  3.34 us (2%)
  loops' own time  1.6 us (1%)
    pallas_call x1, Pallas kernels, exchange(): pl.pallas_call(functools.partial(exchange_kernel, reps, shards), out_shap...  88.6 us
    dot_general x2, matrix products, inverse_root(): jnp.dot(square, square, preferred_element_type=jnp.float32)  9.09 us
    dot_general x2, matrix products, inverse_root(): jnp.dot(current.astype(jnp.bfloat16), factor_low, preferred_element_type=...  6.76 us
    dot_general x1, matrix products, direct_body(): jnp.einsum('kri,kic->krc', half_step, right_root_new, preferred_element_t...  4.94 us
    dot_general x1, matrix products, renew(): jnp.einsum('ci,cj->ij', grad, grad, preferred_element_type=jnp.float32)  3.3 us

profile of v1, /device:TPU:25, one launch (start us, length us, event | category | flops | bytes accessed | tf_op | source)
XLA Modules:
  0.0 135.3 jit_solution(11457569302275211896)
XLA Ops:
  0.6 1.6 %copy.26.left_ref = bf16[3,64,512]{2,1,0:T(8,128)(2,1)} copy(bf16[3,64,512]{2,1,0:T(8,128)(2,1)} %param.14) | data formatting | bytes 393216
  2.2 0.0 copy-start.7
  2.9 0.0 copy-done.7
  2.9 0.6 dynamic_slice.23
  4.2 0.9 dynamic-slice_convert_fusion
  5.1 0.9 dynamic-slice_convert_fusion.1
  6.0 0.7 pad_maximum_fusion.stat_ref
  6.7 88.6 %shard_map.110 = (bf16[3,64,512]{2,1,0:T(8,128)(2,1)}, bf16[3,512,512]{2,1,0:T(8,128)(2,1)S(1)}, bf16[3,512,512]{2,1,0:T(8,128)(2,1)}, bf16[2,512,512]{2,1,0:T(8,128)(2,1)}) custom-call(s32[12]{0:T(128)} %slots_ref.1, bf16[1,3,512,512]{3,2,1,0:T(8,128)(2,1)} %grads_ref.1, bf16[3,64,512]{2,1,0:T(8,128)(2,1)} %copy.26.left_ref, ...), custom_call_target="tpu_custom_call" | custom-call | tf_op jit(solution)/shard_map/pallas_call | solution.py:316
  96.7 0.0 copy-start.1
  96.7 26.5 %conditional.1 = (bf16[512,512]{1,0:T(8,128)(2,1)}, bf16[1,512,512]{2,1,0:T(8,128)(2,1)}, bf16[1,512,512]{2,1,0:T(8,128)(2,1)}) conditional(s32[]{:T(128)} %convert_element_type.72, () %tuple.22, (bf16[2,512,512]{2,1,0:T(8,128)(2,1)}, bf16[3,512,512]{2,1,0:T(8,128)(2,1)S(1)}, s32[]{:T(128)}) %tuple.23), branch_computations={%region_0.1_spmd, %region_1.4_spmd} | conditional | flops 2700607488 | bytes 25166012 | solution.py:393
  96.7 1.6 %convert_element_type.54 = f32[2,512,512]{2,1,0:T(8,128)S(1)} convert(bf16[2,512,512]{2,1,0:T(8,128)(2,1)} %get-tuple-element.17) | non-fusion elementwise | flops 524288 | bytes 3145728 | tf_op jit(solution)/shard_map/cond/branch_1_fun/convert_element_type | solution.py:378
  98.3 0.0 copy-start.2
  98.3 2.3 %multiply_reduce_fusion.1 = (f32[]{:T(128)}, f32[512,512]{1,0:T(8,128)}) fusion(bf16[3,512,512]{2,1,0:T(8,128)(2,1)S(1)} %get-tuple-element.18, s32[]{:T(128)} %get-tuple-element.19, f32[2,512,512]{2,1,0:T(8,128)S(1)} %convert_element_type.54), kind=kOutput, calls=%fused_computation.30 | convolution fusion | flops 270532608 | bytes 2621448 | tf_op jit(solution)/shard_map/cond/branch_1_fun/ic,jc->ij/dot_general | solution.py:381
  100.6 0.0 copy-done.2
  101.3 4.5 %convolution_convert_fusion.4 = bf16[512,512]{1,0:T(8,128)(2,1)} fusion(f32[512,512]{1,0:T(8,128)} %get-tuple-element.40, f32[]{:T(128)S(6)} %div.18), kind=kOutput, calls=%fused_computation.16 | convolution fusion | flops 538968064 | bytes 1572868 | tf_op jit(solution)/shard_map/cond/branch_1_fun/dot_general | solution.py:37
  105.9 3.4 %convolution_convert_fusion.3 = bf16[512,512]{1,0:T(8,128)(2,1)} fusion(bf16[512,512]{1,0:T(8,128)(2,1)} %convolution_convert_fusion.4, f32[512,512]{1,0:T(8,128)} %get-tuple-element.40, f32[]{:T(128)S(6)} %mul.78, f32[]{:T(128)S(6)} %div.18), kind=kOutput, calls=%fused_computation.15 | convolution fusion | flops 540540928 | bytes 2097160 | tf_op jit(solution)/shard_map/cond/branch_1_fun/dot_general | solution.py:30
  109.3 1.9 %copy.18 = bf16[1,512,512]{2,1,0:T(8,128)(2,1)} copy(bf16[1,512,512]{2,1,0:T(8,128)(2,1)} %bitcast.2) | data formatting | bytes 1048576 | tf_op jit(solution)/shard_map/cond
  111.1 3.3 %multiply_reduce_fusion = (f32[]{:T(128)}, f32[512,512]{1,0:T(8,128)}) fusion(bf16[3,512,512]{2,1,0:T(8,128)(2,1)S(1)} %get-tuple-element.18, s32[]{:T(128)} %get-tuple-element.19, f32[2,512,512]{2,1,0:T(8,128)} %copy-done.2), kind=kOutput, calls=%fused_computation.27 | convolution fusion | flops 270532608 | bytes 2621448 | tf_op jit(solution)/shard_map/cond/branch_1_fun/ci,cj->ij/dot_general | solution.py:385
  115.1 4.5 %convolution_convert_fusion.1 = bf16[512,512]{1,0:T(8,128)(2,1)} fusion(f32[512,512]{1,0:T(8,128)} %get-tuple-element.42, f32[]{:T(128)S(6)} %div.20), kind=kOutput, calls=%fused_computation.13 | convolution fusion | flops 538968064 | bytes 1572868 | tf_op jit(solution)/shard_map/cond/branch_1_fun/dot_general | solution.py:37
  119.8 3.4 %fusion.6 = bf16[1,512,512]{2,1,0:T(8,128)(2,1)} fusion(bf16[512,512]{1,0:T(8,128)(2,1)} %convolution_convert_fusion.1, f32[512,512]{1,0:T(8,128)} %get-tuple-element.42, f32[]{:T(128)S(6)} %mul.91, f32[]{:T(128)S(6)} %div.20), kind=kOutput, calls=%fused_computation.20 | convolution fusion | flops 540540928 | bytes 2097160 | tf_op jit(solution)/shard_map/cond/branch_1_fun/dot_general | solution.py:30
  123.2 0.0 copy-done.1
  123.2 2.5 %select_dynamic-update-slice_fusion = (bf16[3,512,512]{2,1,0:T(8,128)(2,1)}, bf16[3,512,512]{2,1,0:T(8,128)(2,1)S(1)}) fusion(bf16[3,512,512]{2,1,0:T(8,128)(2,1)} %get-tuple-element.37, s32[]{:T(128)} %select_n.64, bf16[1,512,512]{2,1,0:T(8,128)(2,1)} %get-tuple-element.38, pred[]{:T(512)S(6)} %eq.20, bf16[3,512,512]{2,1,0:T(8,128)(2,1)S(1)} %copy-done.1, ...), kind=kLoop, calls=%fused_computation.76 | loop fusion | flops 524288 | bytes 3146241 | tf_op jit(solution)/shard_map/jit(_where)/select_n | solution.py:394
  125.6 0.0 copy-start
  125.6 0.0 copy-start.3
  125.6 4.9 %convolution_convert_fusion.6 = bf16[3,512,512]{2,1,0:T(8,128)(2,1)} fusion(bf16[3,512,512]{2,1,0:T(8,128)(2,1)S(1)} %get-tuple-element.44, bf16[3,512,512]{2,1,0:T(8,128)(2,1)} %get-tuple-element.43, bf16[3,512,512]{2,1,0:T(8,128)(2,1)S(1)} %get-tuple-element.33), kind=kOutput, calls=%fused_computation.70 | convolution fusion | flops 1612185600 | bytes 6291456 | tf_op jit(solution)/shard_map/kri,kic->krc/dot_general | solution.py:405
  130.6 0.0 copy-done
  130.6 0.0 copy-start.6
  130.6 0.0 copy-start.5
  130.6 0.0 copy-done.3
  130.6 0.9 fusion.64
  131.5 0.0 copy-start.4
  131.5 2.4 %fusion.61 = f32[3,64,512]{2,1,0:T(8,128)} fusion(bf16[3,512,512]{2,1,0:T(8,128)(2,1)S(1)} %get-tuple-element.33, s32[]{:T(128)S(6)} %select_n.65, f32[3,64,512]{2,1,0:T(8,128)} %param.13), kind=kOutput, calls=%fused_computation.73 | convolution fusion | flops 100958208 | bytes 2752516 | tf_op jit(solution)/shard_map/kic,kij->kcj/dot_general | solution.py:371
  133.9 0.0 copy-done.6
  133.9 0.0 copy-done.5
  133.9 1.3 fusion.62
  135.3 0.0 copy-done.4
Async XLA Ops:
  2.2 0.7 copy-start.7
  96.7 26.5 %copy-start.1 = (bf16[3,512,512]{2,1,0:T(8,128)(2,1)S(1)}, bf16[3,512,512]{2,1,0:T(8,128)(2,1)}, u32[]{:S(2)}) copy-start(bf16[3,512,512]{2,1,0:T(8,128)(2,1)} %param.15) | copy-start | bytes 4718596
  98.3 2.3 %copy-start.2 = (f32[2,512,512]{2,1,0:T(8,128)}, f32[2,512,512]{2,1,0:T(8,128)S(1)}, u32[]{:S(2)}) copy-start(f32[2,512,512]{2,1,0:T(8,128)S(1)} %convert_element_type.54) | copy-start | bytes 6291460 | tf_op jit(solution)/shard_map/cond
  125.6 4.9 %copy-start = (bf16[3,512,512]{2,1,0:T(8,128)(2,1)}, bf16[3,512,512]{2,1,0:T(8,128)(2,1)S(1)}, u32[]{:S(2)}) copy-start(bf16[3,512,512]{2,1,0:T(8,128)(2,1)S(1)} %get-tuple-element.44) | copy-start | bytes 4718596
  125.6 4.9 %copy-start.3 = (bf16[3,64,512]{2,1,0:T(8,128)(2,1)S(1)}, bf16[3,64,512]{2,1,0:T(8,128)(2,1)}, u32[]{:S(2)}) copy-start(bf16[3,64,512]{2,1,0:T(8,128)(2,1)} %copy.26.left_ref) | copy-start | bytes 589828
  130.6 3.3 %copy-start.6 = (bf16[3,64,512]{2,1,0:T(8,128)(2,1)S(1)}, bf16[3,64,512]{2,1,0:T(8,128)(2,1)}, u32[]{:S(2)}) copy-start(bf16[3,64,512]{2,1,0:T(8,128)(2,1)} %get-tuple-element.32) | copy-start | bytes 589828
  130.6 3.3 %copy-start.5 = (f32[3,64,512]{2,1,0:T(8,128)S(1)}, f32[3,64,512]{2,1,0:T(8,128)}, u32[]{:S(2)}) copy-start(f32[3,64,512]{2,1,0:T(8,128)} %param.12) | copy-start | bytes 1179652
  131.5 3.7 %copy-start.4 = (bf16[3,64,512]{2,1,0:T(8,128)(2,1)}, bf16[3,64,512]{2,1,0:T(8,128)(2,1)S(1)}, u32[]{:S(2)}) copy-start(bf16[3,64,512]{2,1,0:T(8,128)(2,1)S(1)} %fusion.64) | copy-start | bytes 589828

commit v2 on v1

--- a/solution.py
+++ b/solution.py
@@ -16,7 +16,10 @@
 
 def inverse_root(statistic):
     order = statistic.shape[0]
-    identity = jnp.eye(order, dtype=jnp.float32)
+    identity = (
+        lax.broadcasted_iota(jnp.int32, (order, order), 0)
+        == lax.broadcasted_iota(jnp.int32, (order, order), 1)
+    ).astype(jnp.float32)
     shifted = statistic + epsilon_shift * identity
     norm_scale = 2.5 / jnp.sqrt(jnp.sum(shifted * shifted))
     moment = norm_scale * shifted
@@ -124,13 +127,16 @@
     reps,
     shards,
     slots_ref,
+    refresh_ref,
     grads_ref,
     left_ref,
-    stat_ref,
+    left_stat_ref,
+    right_stat_ref,
     owned_ref,
     grad_full,
     left_full,
     stat_full,
+    stat_ref,
     pieces,
     share,
     outgoing,
@@ -242,6 +248,9 @@
                     wait_line(array, source, way, delta, None)
                     line_copy(array, source, 2, partner, None).wait_send()
 
+    slot = slots_ref[refresh_ref[0]] % blocks
+    stat_ref[0] = left_stat_ref[slot].astype(jnp.bfloat16)
+    stat_ref[1] = right_stat_ref[slot].astype(jnp.bfloat16)
     begin(0, left_ref)
     begin(1, stat_ref)
     own_left = pltpu.make_async_copy(left_ref, left_full.at[:, span(me), :], local_sem.at[0])
@@ -308,11 +317,12 @@
     return range(1, reps)
 
 
-def exchange(owner_slot, grads, left_root, fresh_stats, reps, shards):
+def exchange(owner_slot, refresh, grads, left_root, left_stat, right_stat, reps, shards):
     blocks, order = grads.shape[1], grads.shape[2]
     rows = order // reps
     low = jnp.bfloat16
     vmem = pl.BlockSpec(memory_space=pltpu.VMEM)
+    smem = pl.BlockSpec(memory_space=pltpu.SMEM)
     return pl.pallas_call(
         functools.partial(exchange_kernel, reps, shards),
         out_shape=(
@@ -321,9 +331,10 @@
             jax.ShapeDtypeStruct((blocks, order, order), low),
             jax.ShapeDtypeStruct((2, order, order), low),
         ),
-        in_specs=[pl.BlockSpec(memory_space=pltpu.SMEM), vmem, vmem, vmem],
+        in_specs=[smem, smem, vmem, vmem, vmem, vmem],
         out_specs=(vmem, vmem, vmem, vmem),
         scratch_shapes=[
+            pltpu.VMEM((2, rows, order), low),
             pltpu.VMEM((reps, blocks, rows, order), low),
             pltpu.VMEM((blocks, rows, order), low),
             pltpu.VMEM((shards, rows, order), low),
@@ -337,75 +348,117 @@
             pltpu.SemaphoreType.DMA((2,)),
         ],
         compiler_params=pltpu.CompilerParams(collective_id=0, has_side_effects=True),
-    )(owner_slot, grads, left_root, fresh_stats)
+    )(owner_slot, refresh, grads, left_root, left_stat, right_stat)
+
+
+def dot(left, right, dims=(1, 0)):
+    return lax.dot_general(
+        left, right, (((dims[0],), (dims[1],)), ((), ())), preferred_element_type=jnp.float32
+    )
+
+
+def precondition_kernel(
+    slots_ref,
+    refresh_ref,
+    owned_ref,
+    grad_full,
+    left_full,
+    stat_full,
+    left_stat_ref,
+    right_stat_ref,
+    left_ref,
+    right_ref,
+    left_new_ref,
+    right_new_ref,
+    left_root_ref,
+    right_root_ref,
+    direction_ref,
+    turned,
+    fresh_left,
+):
+    blocks, rows, order = owned_ref.shape
+    me = lax.axis_index("rep")
+    shard = lax.axis_index("shard")
+    mine = pl.ds(pl.multiple_of(me * rows, rows), rows)
+    fresh_slot = slots_ref[refresh_ref[0]]
+    slot = fresh_slot % blocks
+    owns = fresh_slot // blocks == shard
+    for block in range(blocks):
+        grad = grad_full[block]
+        turned[block] = grad.T
+        left_new_ref[block] = (
+            decay_rate * left_stat_ref[block] + dot(owned_ref[block], grad, (1, 1)) / order
+        )
+        right_new_ref[block] = (
+            decay_rate * right_stat_ref[block] + dot(turned[block, mine, :], grad) / order
+        )
+    left_root_ref[...] = left_ref[...]
+    right_root_ref[...] = right_ref[...]
+
+    @pl.when(owns)
+    def _():
+        grad = grad_full[slot]
+        grad_turned = turned[slot]
+        left = decay_rate * stat_full[0].astype(jnp.float32) + dot(grad, grad_turned) / order
+        right = decay_rate * stat_full[1].astype(jnp.float32) + dot(grad_turned, grad) / order
+        fresh_left[...] = inverse_root(left)
+        left_root_ref[slot] = fresh_left[mine, :]
+        right_root_ref[slot] = inverse_root(right)
+
+    for block in range(blocks):
+        replaced = owns & (slot == block)
+
+        @pl.when(replaced)
+        def _():
+            half = dot(fresh_left[...], grad_full[block]).astype(jnp.bfloat16)
+            direction_ref[block] = half
+
+        @pl.when(jnp.logical_not(replaced))
+        def _():
+            half = dot(left_full[block], grad_full[block]).astype(jnp.bfloat16)
+            direction_ref[block] = half
+
+        direction_ref[block] = dot(direction_ref[block], right_root_ref[block]).astype(
+            jnp.bfloat16
+        )
+
+
+def precondition(*operands):
+    owned, grad_full = operands[2], operands[3]
+    left_stat, left_root, right_root = operands[6], operands[8], operands[9]
+    order = owned.shape[2]
+    low = jnp.bfloat16
+    vmem = pl.BlockSpec(memory_space=pltpu.VMEM)
+    smem = pl.BlockSpec(memory_space=pltpu.SMEM)
+    return pl.pallas_call(
+        precondition_kernel,
+        out_shape=(
+            jax.ShapeDtypeStruct(left_stat.shape, jnp.float32),
+            jax.ShapeDtypeStruct(left_stat.shape, jnp.float32),
+            jax.ShapeDtypeStruct(left_root.shape, low),
+            jax.ShapeDtypeStruct(right_root.shape, low),
+            jax.ShapeDtypeStruct(right_root.shape, low),
+        ),
+        in_specs=[smem, smem] + [vmem] * 8,
+        out_specs=(vmem,) * 5,
+        scratch_shapes=[pltpu.VMEM(grad_full.shape, low), pltpu.VMEM((order, order), low)],
+    )(*operands)
 
 
 def direct_body(grads, owner_slot, refresh, left_stat, right_stat, left_root, right_root):
-    blocks = grads.shape[1]
-    block_order = grads.shape[2]
-    rep_count = lax.axis_size("rep")
-    shards = lax.axis_size("shard")
-    row_count = block_order // rep_count
-    rep_index = lax.axis_index("rep")
-    shard_index = lax.axis_index("shard")
-    fresh_slot = owner_slot[refresh[0]]
-    slot_index = fresh_slot % blocks
-    owns_fresh = fresh_slot // blocks == shard_index
-    fresh_stats = jnp.stack(
-        [
-            lax.dynamic_index_in_dim(left_stat, slot_index, 0, keepdims=False),
-            lax.dynamic_index_in_dim(right_stat, slot_index, 0, keepdims=False),
-        ]
-    ).astype(jnp.bfloat16)
-    owned_rows, gathered, left_full, stat_full = exchange(
-        owner_slot, grads, left_root, fresh_stats, rep_count, shards
-    )
-    left_new = (
-        decay_rate * left_stat
-        + jnp.einsum("krc,kjc->krj", owned_rows, gathered, preferred_element_type=jnp.float32)
-        / block_order
-    )
-    column_share = lax.dynamic_slice_in_dim(gathered, rep_index * row_count, row_count, 2)
-    right_new = (
-        decay_rate * right_stat
-        + jnp.einsum("kic,kij->kcj", column_share, gathered, preferred_element_type=jnp.float32)
-        / block_order
-    )
-    grad_fresh = lax.dynamic_index_in_dim(gathered, slot_index, 0, keepdims=False)
-
-    def renew(operands):
-        grad, stats = operands
-        wide = stats.astype(jnp.float32)
-        left = (
-            decay_rate * wide[0]
-            + jnp.einsum("ic,jc->ij", grad, grad, preferred_element_type=jnp.float32) / block_order
-        )
-        right = (
-            decay_rate * wide[1]
-            + jnp.einsum("ci,cj->ij", grad, grad, preferred_element_type=jnp.float32) / block_order
-        )
-        return inverse_root(left), inverse_root(right)
-
-    def skip(operands):
-        blank = jnp.zeros((block_order, block_order), jnp.bfloat16)
-        return blank, blank
-
-    fresh_left, fresh_right = lax.cond(owns_fresh, renew, skip, (grad_fresh, stat_full))
-    left_all = jnp.where(
-        owns_fresh, lax.dynamic_update_index_in_dim(left_full, fresh_left, slot_index, 0), left_full
-    )
-    fresh_rows = lax.dynamic_slice_in_dim(fresh_left, rep_index * row_count, row_count, 0)
-    left_updated = lax.dynamic_update_index_in_dim(left_root, fresh_rows, slot_index, 0)
-    left_root_new = jnp.where(owns_fresh, left_updated, left_root)
-    right_updated = lax.dynamic_update_index_in_dim(right_root, fresh_right, slot_index, 0)
-    right_root_new = jnp.where(owns_fresh, right_updated, right_root)
-    half_step = jnp.einsum(
-        "kri,kic->krc", left_all, gathered, preferred_element_type=jnp.float32
-    ).astype(jnp.bfloat16)
-    direction = jnp.einsum(
-        "kri,kic->krc", half_step, right_root_new, preferred_element_type=jnp.float32
-    ).astype(jnp.bfloat16)
-    return (left_new, right_new, left_root_new, right_root_new, direction)
+    gathered = exchange(
+        owner_slot,
+        refresh,
+        grads,
+        left_root,
+        left_stat,
+        right_stat,
+        lax.axis_size("rep"),
+        lax.axis_size("shard"),
+    )
+    return precondition(
+        owner_slot, refresh, *gathered, left_stat, right_stat, left_root, right_root
+    )
 
 
 def choose(mesh, *arrays):

time: 135 us -> 102 us (0.76)
  matrix products: 30 us -> 0 us
  Pallas kernels: 88.6 us -> 101 us
  local copies, waits for them, and re-layouts: 5.95 us -> 0 us
  other arithmetic: 5.7 us -> 0 us
  between operations: 3.34 us -> 1.29 us
  loops' own time: 1.6 us -> 0 us
    dot_general x9 -> x0, matrix products: 30 us -> none  [the longest x2 9.09 us: inverse_root(): jnp.dot(square, square, preferred_element_type=jnp.float32)]
    pallas_call x0 -> x1, Pallas kernels: none -> 11.8 us  [precondition(): pl.pallas_call(precondition_kernel, out_shape=(jax.ShapeDtypeStruct(left_...]
    select_n x2 -> x0, other arithmetic: 3.41 us -> none  [the longest x1 2.48 us: direct_body(): jnp.where(owns_fresh, lax.dynamic_update_index_in_dim(left_full, fresh_le...]
    cond x3 -> x0, local copies, waits for them, and re-layouts: 1.87 us -> none
    another operation x2 -> x0, local copies, waits for them, and re-layouts: 1.84 us -> none  [run(): return mapped(mesh, choose(mesh, *arrays))(*arrays)]
    unnamed x15 -> x0, local copies, waits for them, and re-layouts: 1.65 us -> none
    convert_element_type x1 -> x0, other arithmetic: 1.62 us -> none  [renew(): wide = stats.astype(jnp.float32)]
    another operation x1 -> x0, loops' own time: 1.6 us -> none  [direct_body(): lax.cond(owns_fresh, renew, skip, (grad_fresh, stat_full))]
where the time goes in v2:
time: 102 us
  Pallas kernels  101 us (99%)
  between operations  1.29 us (1%)
    pallas_call x1, Pallas kernels, exchange(): pl.pallas_call(functools.partial(exchange_kernel, reps, shards), out_shap...  89.3 us
    pallas_call x1, Pallas kernels, precondition(): pl.pallas_call(precondition_kernel, out_shape=(jax.ShapeDtypeStruct(left_...  11.8 us

profile of v2, /device:TPU:25, one launch (start us, length us, event | category | flops | bytes accessed | tf_op | source)
XLA Modules:
  0.0 102.3 jit_solution(16365944215959458482)
XLA Ops:
  1.3 89.3 %shard_map.110 = (bf16[3,64,512]{2,1,0:T(8,128)(2,1)}, bf16[3,512,512]{2,1,0:T(8,128)(2,1)}, bf16[3,512,512]{2,1,0:T(8,128)(2,1)}, bf16[2,512,512]{2,1,0:T(8,128)(2,1)}) custom-call(s32[12]{0:T(128)} %slots_ref.3, s32[1]{0:T(128)S(6)} %copy.12.refresh_ref, bf16[1,3,512,512]{3,2,1,0:T(8,128)(2,1)} %grads_ref.1, bf16[3,64,512]{2,1,0:T(8,128)(2,1)} %left_ref.3, ...), custom_call_target="tpu_custom_call" | custom-call | tf_op jit(solution)/shard_map/pallas_call | solution.py:326
  90.6 11.8 %shard_map.111 = (f32[3,64,512]{2,1,0:T(8,128)}, f32[3,64,512]{2,1,0:T(8,128)}, bf16[3,64,512]{2,1,0:T(8,128)(2,1)}, bf16[3,512,512]{2,1,0:T(8,128)(2,1)}, bf16[3,512,512]{2,1,0:T(8,128)(2,1)}) custom-call(s32[12]{0:T(128)} %slots_ref.3, s32[1]{0:T(128)S(6)} %copy.12.refresh_ref, bf16[3,64,512]{2,1,0:T(8,128)(2,1)} %get-tuple-element.9.owned_ref, ...), custom_call_target="tpu_custom_call" | custom-call | tf_op jit(solution)/shard_map/pallas_call | solution.py:433

commit v3 on v2

--- a/solution.py
+++ b/solution.py
@@ -137,6 +137,8 @@
     left_full,
     stat_full,
     stat_ref,
+    quarter_in,
+    quarter,
     pieces,
     share,
     outgoing,
@@ -145,6 +147,10 @@
     sum_recv,
     swap_send,
     swap_recv,
+    part_send,
+    part_recv,
+    spread_send,
+    spread_recv,
     line_send,
     line_recv,
     local_sem,
@@ -161,6 +167,14 @@
     def span(index):
         return pl.ds(pl.multiple_of(index * rows, rows), rows)
 
+    slot = slots_ref[refresh_ref[0]] % blocks
+    keeper = slots_ref[refresh_ref[0]] // blocks
+    part = rows // shards
+    for index in range(shards):
+        part_rows = pl.ds(index * part, part)
+        stat_ref[index, 0] = left_stat_ref[slot, part_rows, :].astype(jnp.bfloat16)
+        stat_ref[index, 1] = right_stat_ref[slot, part_rows, :].astype(jnp.bfloat16)
+
     barrier = pltpu.get_barrier_semaphore()
     for step in range(1, reps):
         pl.semaphore_signal(
@@ -172,28 +186,51 @@
         )
     pl.semaphore_wait(barrier, reps + shards - 2)
 
+    def to_shards(source, target, send_sem, recv_sem):
+        copies = []
+        for step in range(1, shards):
+            peer = (shard + step) % shards
+            copies.append(
+                pltpu.make_async_remote_copy(
+                    src_ref=source(peer),
+                    dst_ref=target,
+                    send_sem=send_sem.at[step],
+                    recv_sem=recv_sem.at[step],
+                    device_id=(me, peer),
+                    device_id_type=MESH,
+                )
+            )
+        return copies
+
     sums = []
-    for step in SUM_ORDER(reps):
-        peer = (me + step) % reps
-        copy = pltpu.make_async_remote_copy(
-            src_ref=grads_ref.at[0, :, span(peer), :],
-            dst_ref=pieces.at[me],
-            send_sem=sum_send.at[step],
-            recv_sem=sum_recv.at[step],
-            device_id=(peer, shard),
-            device_id_type=MESH,
-        )
-        copy.start()
-        sums.append(copy)
+
+    def send_sums(steps):
+        for step in steps:
+            peer = (me + step) % reps
+            copy = pltpu.make_async_remote_copy(
+                src_ref=grads_ref.at[0, :, span(peer), :],
+                dst_ref=pieces.at[me],
+                send_sem=sum_send.at[step],
+                recv_sem=sum_recv.at[step],
+                device_id=(peer, shard),
+                device_id_type=MESH,
+            )
+            copy.start()
+            sums.append(copy)
 
     fulls = (left_full, stat_full, grad_full)
 
+    def spots(array, source):
+        if array == 1:
+            return stat_full.at[:, source, shard]
+        return fulls[array].at[:, span(source), :]
+
     def line_copy(array, source, way, target, first):
-        full = fulls[array]
-        origin = first if first is not None else full.at[:, span(source), :]
+        where = spots(array, source)
+        origin = first if first is not None else where
         return pltpu.make_async_remote_copy(
             src_ref=origin,
-            dst_ref=full.at[:, span(source), :],
+            dst_ref=where,
             send_sem=line_send.at[array, source, way],
             recv_sem=line_recv.at[array, source],
             device_id=(target, shard),
@@ -233,8 +270,9 @@
                 line_copy(array, source, 2, partner, None).start()
 
     def finish(array, first):
-        for other in range(length):
-            line_copy(array, other * 2 + 1 - side, 2, partner, None).wait_recv()
+        if array != 1:
+            for other in range(length):
+                line_copy(array, other * 2 + 1 - side, 2, partner, None).wait_recv()
         for way, delta in ways:
             wait_line(array, me, way, delta, first)
         line_copy(array, me, 2, partner, first).wait_send()
@@ -248,15 +286,28 @@
                     wait_line(array, source, way, delta, None)
                     line_copy(array, source, 2, partner, None).wait_send()
 
-    slot = slots_ref[refresh_ref[0]] % blocks
-    stat_ref[0] = left_stat_ref[slot].astype(jnp.bfloat16)
-    stat_ref[1] = right_stat_ref[slot].astype(jnp.bfloat16)
+    parts = to_shards(lambda peer: stat_ref.at[peer], quarter_in.at[shard], part_send, part_recv)
+    for copy in parts:
+        copy.start()
     begin(0, left_ref)
-    begin(1, stat_ref)
-    own_left = pltpu.make_async_copy(left_ref, left_full.at[:, span(me), :], local_sem.at[0])
+    own_left = pltpu.make_async_copy(left_ref, spots(0, me), local_sem.at[0])
     own_left.start()
-    own_stat = pltpu.make_async_copy(stat_ref, stat_full.at[:, span(me), :], local_sem.at[1])
+    send_sums(range(1, min(4, reps)))
+    quarter_in[shard] = stat_ref[shard]
+    for copy in parts:
+        copy.wait_recv()
+    quarter[...] = quarter_in[keeper]
+    begin(1, quarter)
+    own_stat = pltpu.make_async_copy(quarter, spots(1, me), local_sem.at[1])
     own_stat.start()
+    send_sums(range(4, min(6, reps)))
+    if length > 1:
+        forward(1, 1)
+        forward(0, 1)
+    send_sums(range(6, reps))
+    if length > 2:
+        forward(1, 2)
+        forward(0, 2)
 
     pieces[me] = grads_ref[0, :, span(me), :]
     for copy in sums:
@@ -274,19 +325,9 @@
                 slots_ref[shard * blocks + block] // blocks == target, jnp.int32(block), chosen
             )
         outgoing[target] = share[chosen]
-    swaps = []
-    for step in range(1, shards):
-        peer = (shard + step) % shards
-        copy = pltpu.make_async_remote_copy(
-            src_ref=outgoing.at[peer],
-            dst_ref=incoming.at[shard],
-            send_sem=swap_send.at[step],
-            recv_sem=swap_recv.at[step],
-            device_id=(me, peer),
-            device_id_type=MESH,
-        )
+    swaps = to_shards(lambda peer: outgoing.at[peer], incoming.at[shard], swap_send, swap_recv)
+    for copy in swaps:
         copy.start()
-        swaps.append(copy)
     incoming[shard] = outgoing[shard]
     for copy in swaps:
         copy.wait_recv()
@@ -300,21 +341,30 @@
             )
         value = incoming[holder]
         owned_ref[block] = value
-        grad_full[block, span(me), :] = value
     begin(2, owned_ref)
+    own_grad = pltpu.make_async_copy(owned_ref, spots(2, me), local_sem.at[2])
+    own_grad.start()
+    for hop in range(3, length):
+        forward(1, hop)
+        forward(0, hop)
+    own_stat.wait()
+    for other in range(length):
+        line_copy(1, other * 2 + 1 - side, 2, partner, None).wait_recv()
+    spreads = to_shards(
+        lambda peer: stat_full.at[:, :, shard], stat_full.at[:, :, shard], spread_send, spread_recv
+    )
+    for copy in spreads:
+        copy.start()
     for hop in range(1, length):
-        for array in range(3):
-            forward(array, hop)
-    for array, first in enumerate((left_ref, stat_ref, owned_ref)):
+        forward(2, hop)
+    for array, first in enumerate((left_ref, quarter, owned_ref)):
         finish(array, first)
     own_left.wait()
-    own_stat.wait()
-    for copy in sums + swaps:
+    own_grad.wait()
+    for copy in spreads:
+        copy.wait_recv()
+    for copy in sums + swaps + parts + spreads:
         copy.wait_send()
-
-
-def SUM_ORDER(reps):
-    return range(1, reps)
 
 
 def exchange(owner_slot, refresh, grads, left_root, left_stat, right_stat, reps, shards):
@@ -323,18 +373,21 @@
     low = jnp.bfloat16
     vmem = pl.BlockSpec(memory_space=pltpu.VMEM)
     smem = pl.BlockSpec(memory_space=pltpu.SMEM)
+    hbm = pl.BlockSpec(memory_space=pl.ANY)
     return pl.pallas_call(
         functools.partial(exchange_kernel, reps, shards),
         out_shape=(
             jax.ShapeDtypeStruct((blocks, rows, order), low),
             jax.ShapeDtypeStruct((blocks, order, order), low),
             jax.ShapeDtypeStruct((blocks, order, order), low),
-            jax.ShapeDtypeStruct((2, order, order), low),
+            jax.ShapeDtypeStruct((2, reps, shards, rows // shards, order), low),
         ),
         in_specs=[smem, smem, vmem, vmem, vmem, vmem],
-        out_specs=(vmem, vmem, vmem, vmem),
+        out_specs=(vmem, hbm, hbm, hbm),
         scratch_shapes=[
-            pltpu.VMEM((2, rows, order), low),
+            pltpu.VMEM((shards, 2, rows // shards, order), low),
+            pltpu.VMEM((shards, 2, rows // shards, order), low),
+            pltpu.VMEM((2, rows // shards, order), low),
             pltpu.VMEM((reps, blocks, rows, order), low),
             pltpu.VMEM((blocks, rows, order), low),
             pltpu.VMEM((shards, rows, order), low),
@@ -343,9 +396,13 @@
             pltpu.SemaphoreType.DMA((reps,)),
             pltpu.SemaphoreType.DMA((shards,)),
             pltpu.SemaphoreType.DMA((shards,)),
+            pltpu.SemaphoreType.DMA((shards,)),
+            pltpu.SemaphoreType.DMA((shards,)),
+            pltpu.SemaphoreType.DMA((shards,)),
+            pltpu.SemaphoreType.DMA((shards,)),
             pltpu.SemaphoreType.DMA((3, reps, 3)),
             pltpu.SemaphoreType.DMA((3, reps)),
-            pltpu.SemaphoreType.DMA((2,)),
+            pltpu.SemaphoreType.DMA((3,)),
         ],
         compiler_params=pltpu.CompilerParams(collective_id=0, has_side_effects=True),
     )(owner_slot, refresh, grads, left_root, left_stat, right_stat)
@@ -446,7 +503,7 @@
 
 
 def direct_body(grads, owner_slot, refresh, left_stat, right_stat, left_root, right_root):
-    gathered = exchange(
+    owned, grad_full, left_full, stat_full = exchange(
         owner_slot,
         refresh,
         grads,
@@ -456,6 +513,9 @@
         lax.axis_size("rep"),
         lax.axis_size("shard"),
     )
+    order = grads.shape[2]
+    stat_full = stat_full.reshape(2, order, order)
+    gathered = (owned, grad_full, left_full, stat_full)
     return precondition(
         owner_slot, refresh, *gathered, left_stat, right_stat, left_root, right_root
     )
@@ -464,7 +524,7 @@
 def choose(mesh, *arrays):
     reps = mesh.shape["rep"]
     rows = arrays[0].shape[2] // reps
-    direct = reps % 2 == 0 and rows % 16 == 0
+    direct = reps % 2 == 0 and rows % (16 * mesh.shape["shard"]) == 0
     return (direct_body if direct else body)
 
 

time: 102 us -> 103 us (level)
  the two profiles are of different devices: /device:TPU:25 before, /device:TPU:0 now
where the time goes in v3:
time: 103 us
  Pallas kernels  101 us (98%)
  between operations  1.29 us (1%)
    pallas_call x1, Pallas kernels, exchange(): pl.pallas_call(functools.partial(exchange_kernel, reps, shards), out_shap...  89.5 us
    pallas_call x1, Pallas kernels, precondition(): pl.pallas_call(precondition_kernel, out_shape=(jax.ShapeDtypeStruct(left_...  11.7 us

profile of v3, /device:TPU:0, one launch (start us, length us, event | category | flops | bytes accessed | tf_op | source)
XLA Modules:
  0.0 102.6 jit_solution(5511690629646990099)
XLA Ops:
  1.3 89.5 %shard_map.110 = (bf16[3,64,512]{2,1,0:T(8,128)(2,1)}, bf16[3,512,512]{2,1,0:T(8,128)(2,1)}, bf16[3,512,512]{2,1,0:T(8,128)(2,1)}, bf16[2,8,4,16,512]{4,3,2,1,0:T(8,128)(2,1)}) custom-call(s32[12]{0:T(128)} %slots_ref.3, s32[1]{0:T(128)S(6)} %copy.12.refresh_ref, bf16[1,3,512,512]{3,2,1,0:T(8,128)(2,1)} %grads_ref.1, bf16[3,64,512]{2,1,0:T(8,128)(2,1)} %left_ref.3, ...), custom_call_target="tpu_custom_call" | custom-call | tf_op jit(solution)/shard_map/pallas_call | solution.py:377
  90.8 11.7 %shard_map.111 = (f32[3,64,512]{2,1,0:T(8,128)}, f32[3,64,512]{2,1,0:T(8,128)}, bf16[3,64,512]{2,1,0:T(8,128)(2,1)}, bf16[3,512,512]{2,1,0:T(8,128)(2,1)}, bf16[3,512,512]{2,1,0:T(8,128)(2,1)}) custom-call(s32[12]{0:T(128)} %slots_ref.3, s32[1]{0:T(128)S(6)} %copy.12.refresh_ref, bf16[3,64,512]{2,1,0:T(8,128)(2,1)} %get-tuple-element.9.owned_ref, ...), custom_call_target="tpu_custom_call" | custom-call | tf_op jit(solution)/shard_map/pallas_call | solution.py:490

commit v4 on v3

--- a/solution.py
+++ b/solution.py
@@ -132,16 +132,20 @@
     left_ref,
     left_stat_ref,
     right_stat_ref,
-    owned_ref,
     grad_full,
     left_full,
+    left_new_ref,
+    right_new_ref,
+    fresh_left_ref,
+    fresh_right_ref,
+    owned_ref,
     stat_full,
+    turned,
     stat_ref,
     quarter_in,
     quarter,
     pieces,
     share,
-    outgoing,
     incoming,
     sum_send,
     sum_recv,
@@ -156,7 +160,8 @@
     local_sem,
 ):
     blocks = grads_ref.shape[1]
-    rows = grads_ref.shape[2] // reps
+    order = grads_ref.shape[2]
+    rows = order // reps
     length = reps // 2
     me = lax.axis_index("rep")
     shard = lax.axis_index("shard")
@@ -202,28 +207,28 @@
             )
         return copies
 
-    sums = []
-
-    def send_sums(steps):
-        for step in steps:
+    sums = [[] for block in range(blocks)]
+
+    def send_sums(block):
+        for step in range(1, reps):
             peer = (me + step) % reps
             copy = pltpu.make_async_remote_copy(
-                src_ref=grads_ref.at[0, :, span(peer), :],
-                dst_ref=pieces.at[me],
-                send_sem=sum_send.at[step],
-                recv_sem=sum_recv.at[step],
+                src_ref=grads_ref.at[0, block, span(peer), :],
+                dst_ref=pieces.at[me, block],
+                send_sem=sum_send.at[block, step],
+                recv_sem=sum_recv.at[block, step],
                 device_id=(peer, shard),
                 device_id_type=MESH,
             )
             copy.start()
-            sums.append(copy)
-
-    fulls = (left_full, stat_full, grad_full)
+            sums[block].append(copy)
 
     def spots(array, source):
         if array == 1:
             return stat_full.at[:, source, shard]
-        return fulls[array].at[:, span(source), :]
+        if array == 0:
+            return left_full.at[:, span(source), :]
+        return grad_full.at[array - 2, span(source), :]
 
     def line_copy(array, source, way, target, first):
         where = spots(array, source)
@@ -270,7 +275,7 @@
                 line_copy(array, source, 2, partner, None).start()
 
     def finish(array, first):
-        if array != 1:
+        if array == 0:
             for other in range(length):
                 line_copy(array, other * 2 + 1 - side, 2, partner, None).wait_recv()
         for way, delta in ways:
@@ -289,10 +294,11 @@
     parts = to_shards(lambda peer: stat_ref.at[peer], quarter_in.at[shard], part_send, part_recv)
     for copy in parts:
         copy.start()
+    for block in range(blocks):
+        send_sums(block)
     begin(0, left_ref)
     own_left = pltpu.make_async_copy(left_ref, spots(0, me), local_sem.at[0])
     own_left.start()
-    send_sums(range(1, min(4, reps)))
     quarter_in[shard] = stat_ref[shard]
     for copy in parts:
         copy.wait_recv()
@@ -300,53 +306,48 @@
     begin(1, quarter)
     own_stat = pltpu.make_async_copy(quarter, spots(1, me), local_sem.at[1])
     own_stat.start()
-    send_sums(range(4, min(6, reps)))
-    if length > 1:
-        forward(1, 1)
-        forward(0, 1)
-    send_sums(range(6, reps))
-    if length > 2:
-        forward(1, 2)
-        forward(0, 2)
-
     pieces[me] = grads_ref[0, :, span(me), :]
-    for copy in sums:
-        copy.wait_recv()
-    for block in range(blocks):
+    swaps = []
+
+    def add_up(block):
+        for copy in sums[block]:
+            copy.wait_recv()
         total = pieces[0, block].astype(jnp.float32)
         for index in range(1, reps):
             total = total + pieces[index, block].astype(jnp.float32)
         share[block] = total.astype(jnp.bfloat16)
-
-    for target in range(shards):
-        chosen = jnp.int32(0)
-        for block in range(1, blocks):
-            chosen = jnp.where(
-                slots_ref[shard * blocks + block] // blocks == target, jnp.int32(block), chosen
-            )
-        outgoing[target] = share[chosen]
-    swaps = to_shards(lambda peer: outgoing.at[peer], incoming.at[shard], swap_send, swap_recv)
-    for copy in swaps:
-        copy.start()
-    incoming[shard] = outgoing[shard]
-    for copy in swaps:
-        copy.wait_recv()
+        copies = to_shards(
+            lambda peer: share.at[block],
+            incoming.at[block, shard],
+            swap_send.at[block],
+            swap_recv.at[block],
+        )
+        for copy in copies:
+            copy.start()
+        swaps.append(copies)
+        incoming[block, shard] = share[block]
+
+    def take(block):
+        for copy in swaps[block]:
+            copy.wait_recv()
+        value = incoming[block, 0]
+        for origin in range(1, shards):
+            held = slots_ref[origin * blocks + block] == shard * blocks + block
+            value = jnp.where(held, incoming[block, origin], value)
+        owned_ref[block] = value
+        begin(2 + block, owned_ref.at[block])
+
     for block in range(blocks):
-        holder = jnp.int32(0)
-        for origin in range(1, shards):
-            holder = jnp.where(
-                slots_ref[origin * blocks + block] == shard * blocks + block,
-                jnp.int32(origin),
-                holder,
-            )
-        value = incoming[holder]
-        owned_ref[block] = value
-    begin(2, owned_ref)
-    own_grad = pltpu.make_async_copy(owned_ref, spots(2, me), local_sem.at[2])
+        add_up(block)
+        if block > 0:
+            take(block - 1)
+    take(blocks - 1)
+    own_grad = pltpu.make_async_copy(owned_ref, grad_full.at[:, span(me), :], local_sem.at[2])
     own_grad.start()
-    for hop in range(3, length):
+    for hop in range(1, length):
         forward(1, hop)
-        forward(0, hop)
+        for array in range(2, 2 + blocks):
+            forward(array, hop)
     own_stat.wait()
     for other in range(length):
         line_copy(1, other * 2 + 1 - side, 2, partner, None).wait_recv()
@@ -355,16 +356,41 @@
     )
     for copy in spreads:
         copy.start()
-    for hop in range(1, length):
-        forward(2, hop)
-    for array, first in enumerate((left_ref, quarter, owned_ref)):
-        finish(array, first)
-    own_left.wait()
     own_grad.wait()
+    if length > 1:
+        forward(0, 1)
+    for block in range(blocks):
+        for other in range(length):
+            line_copy(2 + block, other * 2 + 1 - side, 2, partner, None).wait_recv()
+    if length > 2:
+        forward(0, 2)
+    for block in range(blocks):
+        grad = grad_full[block]
+        turned[block] = grad.T
+        left_new_ref[block] = (
+            decay_rate * left_stat_ref[block] + dot(owned_ref[block], grad, (1, 1)) / order
+        )
+        right_new_ref[block] = (
+            decay_rate * right_stat_ref[block] + dot(turned[block, span(me), :], grad) / order
+        )
+    for hop in range(3, length):
+        forward(0, hop)
     for copy in spreads:
         copy.wait_recv()
-    for copy in sums + swaps + parts + spreads:
-        copy.wait_send()
+    grad = grad_full[slot]
+    grad_turned = turned[slot]
+    left_sum = stat_full[0].reshape(order, order).astype(jnp.float32)
+    right_sum = stat_full[1].reshape(order, order).astype(jnp.float32)
+    fresh_left_ref[...] = inverse_root(decay_rate * left_sum + dot(grad, grad_turned) / order)
+    fresh_right_ref[...] = inverse_root(decay_rate * right_sum + dot(grad_turned, grad) / order)
+    finish(0, left_ref)
+    finish(1, quarter)
+    for block in range(blocks):
+        finish(2 + block, owned_ref.at[block])
+    own_left.wait()
+    for copies in sums + swaps + [parts, spreads]:
+        for copy in copies:
+            copy.wait_send()
 
 
 def exchange(owner_slot, refresh, grads, left_root, left_stat, right_stat, reps, shards):
@@ -377,31 +403,35 @@
     return pl.pallas_call(
         functools.partial(exchange_kernel, reps, shards),
         out_shape=(
-            jax.ShapeDtypeStruct((blocks, rows, order), low),
             jax.ShapeDtypeStruct((blocks, order, order), low),
             jax.ShapeDtypeStruct((blocks, order, order), low),
-            jax.ShapeDtypeStruct((2, reps, shards, rows // shards, order), low),
+            jax.ShapeDtypeStruct((blocks, rows, order), jnp.float32),
+            jax.ShapeDtypeStruct((blocks, rows, order), jnp.float32),
+            jax.ShapeDtypeStruct((order, order), low),
+            jax.ShapeDtypeStruct((order, order), low),
         ),
         in_specs=[smem, smem, vmem, vmem, vmem, vmem],
-        out_specs=(vmem, hbm, hbm, hbm),
+        out_specs=(vmem, hbm, vmem, vmem, vmem, vmem),
         scratch_shapes=[
+            pltpu.VMEM((blocks, rows, order), low),
+            pltpu.VMEM((2, reps, shards, rows // shards, order), low),
+            pltpu.VMEM((blocks, order, order), low),
             pltpu.VMEM((shards, 2, rows // shards, order), low),
             pltpu.VMEM((shards, 2, rows // shards, order), low),
             pltpu.VMEM((2, rows // shards, order), low),
             pltpu.VMEM((reps, blocks, rows, order), low),
             pltpu.VMEM((blocks, rows, order), low),
-            pltpu.VMEM((shards, rows, order), low),
-            pltpu.VMEM((shards, rows, order), low),
-            pltpu.SemaphoreType.DMA((reps,)),
-            pltpu.SemaphoreType.DMA((reps,)),
+            pltpu.VMEM((blocks, shards, rows, order), low),
+            pltpu.SemaphoreType.DMA((blocks, reps)),
+            pltpu.SemaphoreType.DMA((blocks, reps)),
+            pltpu.SemaphoreType.DMA((blocks, shards)),
+            pltpu.SemaphoreType.DMA((blocks, shards)),
             pltpu.SemaphoreType.DMA((shards,)),
             pltpu.SemaphoreType.DMA((shards,)),
             pltpu.SemaphoreType.DMA((shards,)),
             pltpu.SemaphoreType.DMA((shards,)),
-            pltpu.SemaphoreType.DMA((shards,)),
-            pltpu.SemaphoreType.DMA((shards,)),
-            pltpu.SemaphoreType.DMA((3, reps, 3)),
-            pltpu.SemaphoreType.DMA((3, reps)),
+            pltpu.SemaphoreType.DMA((2 + blocks, reps, 3)),
+            pltpu.SemaphoreType.DMA((2 + blocks, reps)),
             pltpu.SemaphoreType.DMA((3,)),
         ],
         compiler_params=pltpu.CompilerParams(collective_id=0, has_side_effects=True),
@@ -417,63 +447,41 @@
 def precondition_kernel(
     slots_ref,
     refresh_ref,
-    owned_ref,
     grad_full,
     left_full,
-    stat_full,
-    left_stat_ref,
-    right_stat_ref,
+    new_left_ref,
+    new_right_ref,
     left_ref,
     right_ref,
-    left_new_ref,
-    right_new_ref,
     left_root_ref,
     right_root_ref,
     direction_ref,
-    turned,
-    fresh_left,
 ):
-    blocks, rows, order = owned_ref.shape
+    blocks, rows, order = left_ref.shape
     me = lax.axis_index("rep")
     shard = lax.axis_index("shard")
     mine = pl.ds(pl.multiple_of(me * rows, rows), rows)
     fresh_slot = slots_ref[refresh_ref[0]]
     slot = fresh_slot % blocks
     owns = fresh_slot // blocks == shard
-    for block in range(blocks):
-        grad = grad_full[block]
-        turned[block] = grad.T
-        left_new_ref[block] = (
-            decay_rate * left_stat_ref[block] + dot(owned_ref[block], grad, (1, 1)) / order
-        )
-        right_new_ref[block] = (
-            decay_rate * right_stat_ref[block] + dot(turned[block, mine, :], grad) / order
-        )
     left_root_ref[...] = left_ref[...]
     right_root_ref[...] = right_ref[...]
 
     @pl.when(owns)
     def _():
-        grad = grad_full[slot]
-        grad_turned = turned[slot]
-        left = decay_rate * stat_full[0].astype(jnp.float32) + dot(grad, grad_turned) / order
-        right = decay_rate * stat_full[1].astype(jnp.float32) + dot(grad_turned, grad) / order
-        fresh_left[...] = inverse_root(left)
-        left_root_ref[slot] = fresh_left[mine, :]
-        right_root_ref[slot] = inverse_root(right)
+        left_root_ref[slot] = new_left_ref[mine, :]
+        right_root_ref[slot] = new_right_ref[...]
 
     for block in range(blocks):
         replaced = owns & (slot == block)
 
         @pl.when(replaced)
         def _():
-            half = dot(fresh_left[...], grad_full[block]).astype(jnp.bfloat16)
-            direction_ref[block] = half
+            direction_ref[block] = dot(new_left_ref[...], grad_full[block]).astype(jnp.bfloat16)
 
         @pl.when(jnp.logical_not(replaced))
         def _():
-            half = dot(left_full[block], grad_full[block]).astype(jnp.bfloat16)
-            direction_ref[block] = half
+            direction_ref[block] = dot(left_full[block], grad_full[block]).astype(jnp.bfloat16)
 
         direction_ref[block] = dot(direction_ref[block], right_root_ref[block]).astype(
             jnp.bfloat16
@@ -481,29 +489,24 @@
 
 
 def precondition(*operands):
-    owned, grad_full = operands[2], operands[3]
-    left_stat, left_root, right_root = operands[6], operands[8], operands[9]
-    order = owned.shape[2]
+    left_root, right_root = operands[6], operands[7]
     low = jnp.bfloat16
     vmem = pl.BlockSpec(memory_space=pltpu.VMEM)
     smem = pl.BlockSpec(memory_space=pltpu.SMEM)
     return pl.pallas_call(
         precondition_kernel,
         out_shape=(
-            jax.ShapeDtypeStruct(left_stat.shape, jnp.float32),
-            jax.ShapeDtypeStruct(left_stat.shape, jnp.float32),
             jax.ShapeDtypeStruct(left_root.shape, low),
             jax.ShapeDtypeStruct(right_root.shape, low),
             jax.ShapeDtypeStruct(right_root.shape, low),
         ),
-        in_specs=[smem, smem] + [vmem] * 8,
-        out_specs=(vmem,) * 5,
-        scratch_shapes=[pltpu.VMEM(grad_full.shape, low), pltpu.VMEM((order, order), low)],
+        in_specs=[smem, smem] + [vmem] * 6,
+        out_specs=(vmem,) * 3,
     )(*operands)
 
 
 def direct_body(grads, owner_slot, refresh, left_stat, right_stat, left_root, right_root):
-    owned, grad_full, left_full, stat_full = exchange(
+    grad_full, left_full, left_new, right_new, fresh_left, fresh_right = exchange(
         owner_slot,
         refresh,
         grads,
@@ -513,12 +516,10 @@
         lax.axis_size("rep"),
         lax.axis_size("shard"),
     )
-    order = grads.shape[2]
-    stat_full = stat_full.reshape(2, order, order)
-    gathered = (owned, grad_full, left_full, stat_full)
-    return precondition(
-        owner_slot, refresh, *gathered, left_stat, right_stat, left_root, right_root
-    )
+    roots = precondition(
+        owner_slot, refresh, grad_full, left_full, fresh_left, fresh_right, left_root, right_root
+    )
+    return (left_new, right_new, *roots)
 
 
 def choose(mesh, *arrays):

time: 103 us -> 91.2 us (0.89)
  the two profiles are of different devices: /device:TPU:0 before, /device:TPU:25 now
where the time goes in v4:
time: 91.2 us; the launch traced here: 90.7 us
  Pallas kernels  87.9 us (96%)
  local copies, waits for them, and re-layouts  1.5 us (2%)
  between operations  1.3 us (1%)
    pallas_call x1, Pallas kernels, exchange(): pl.pallas_call(functools.partial(exchange_kernel, reps, shards), out_shap...  81 us
    pallas_call x1, Pallas kernels, precondition(): pl.pallas_call(precondition_kernel, out_shape=(jax.ShapeDtypeStruct(left_...  6.87 us

profile of v4, /device:TPU:25, one launch (start us, length us, event | category | flops | bytes accessed | tf_op | source)
XLA Modules:
  0.0 90.7 jit_solution(414737004235189897)
XLA Ops:
  1.3 81.0 %shard_map.110 = (bf16[3,512,512]{2,1,0:T(8,128)(2,1)}, bf16[3,512,512]{2,1,0:T(8,128)(2,1)}, f32[3,64,512]{2,1,0:T(8,128)}, f32[3,64,512]{2,1,0:T(8,128)}, bf16...) custom-call(s32[12]{0:T(128)} %slots_ref.3, s32[1]{0:T(128)S(6)} %copy.14.refresh_ref, bf16[1,3,512,512]{3,2,1,0:T(8,128)(2,1)} %grads_ref.1, ...), custom_call_target="tpu_custom_call" | custom-call | tf_op jit(solution)/shard_map/pallas_call | solution.py:403
  82.3 0.0 copy-start.1
  82.3 0.0 copy-start
  82.3 6.9 %shard_map.111 = (bf16[3,64,512]{2,1,0:T(8,128)(2,1)}, bf16[3,512,512]{2,1,0:T(8,128)(2,1)}, bf16[3,512,512]{2,1,0:T(8,128)(2,1)}) custom-call(s32[12]{0:T(128)} %slots_ref.3, s32[1]{0:T(128)S(6)} %copy.14.refresh_ref, bf16[3,512,512]{2,1,0:T(8,128)(2,1)} %get-tuple-element.16.grad_full, bf16[3,512,512]{2,1,0:T(8,128)(2,1)} %get-tuple-element.17.left_full, ...), custom_call_target="tpu_custom_call" | custom-call | tf_op jit(solution)/shard_map/pallas_call | solution.py:496
  89.2 0.0 copy-done.1
  89.2 0.7 copy.15
  89.9 0.0 copy-done
  89.9 0.7 copy.16
Async XLA Ops:
  82.3 6.9 %copy-start.1 = (f32[3,64,512]{2,1,0:T(8,128)S(1)}, f32[3,64,512]{2,1,0:T(8,128)}, u32[]{:S(2)}) copy-start(f32[3,64,512]{2,1,0:T(8,128)} %get-tuple-element.28) | copy-start | bytes 1179652
  82.3 7.6 %copy-start = (f32[3,64,512]{2,1,0:T(8,128)S(1)}, f32[3,64,512]{2,1,0:T(8,128)}, u32[]{:S(2)}) copy-start(f32[3,64,512]{2,1,0:T(8,128)} %get-tuple-element.29) | copy-start | bytes 1179652
